TPU v7x, 512 devices: a whole 4x4x16 slice. The times are simulated.
512 devices in a mesh: seq: 16 (over y, x), table: 32 (over z, core).
Axes of the slice: x: 4, y: 4, z: 16, core: 2. Of those that a mesh axis runs over, the one named last changes fastest.
Arguments:
- events_x: bfloat16 [32, 2048, 512], P('table', 'seq'), may hold values from -6 to 6
- proj: bfloat16 [512, 1536], replicated, may hold values from -0.25 to 0.25
- out_grad: bfloat16 [32, 2048, 512], P('table', 'seq'), may hold values from -6 to 6
- block_mask: int32 [16, 16], replicated, may hold values 0 or 1
- item_ids: int32 [32, 2048], P('table', 'seq'), may hold values from 0 to 16383, as said below
- owner_of: int32 [16384], replicated, may hold values from 0 to 31, as said below
- local_of: int32 [16384], replicated, may hold values from 0 to 511, as said below
- table: bfloat16 [16384, 512], P('table'), may hold values from -3 to 3
- moment: float32 [16384, 512], P('table'), may hold values from -2 to 2
- second: float32 [16384], P('table'), may hold values from 0.05 to 2
Outputs:
- new_table: bfloat16 [16384, 512], P('table')
- new_moment: float32 [16384, 512], P('table')
- new_second: float32 [16384], P('table')
- event_rows: bfloat16 [32, 2048, 512], P('table', 'seq')
Inputs may be any that keep to these rules, and one draw needn't show every extreme that they name: `item_ids`: among the 128 events of one device (one history, one seq index), at most 8 have items of one owner (owner_of); in every draw, for each seq index, some owner gets exactly 8 from the device of every history. owner_of[r] * 512 + local_of[r] takes every value of 0 to 16383 once over the items r. `local_of`: see owner_of.
All inputs are finite; a program needn't handle non-finite values.
Results may differ from a plain program's by a relative error of at most 0.0075.
Values may be sent and summed in bfloat16 or wider, within the bound.
No kernel may reach another device: no remote copies, remote signals or barrier semaphores. Data moves between devices by JAX's collectives and lax.ppermute only.
A program may use at most 64 MiB of HBM per device.

v0:
```python
import math
import jax
import jax.numpy as jnp
from jax import lax
from jax.sharding import PartitionSpec as P

HEADS = 8
first_decay = 0.9
second_decay = 0.99
step_rate = 0.05
epsilon = 1e-08


def block_length(piece_rows):
    block_rows = piece_rows
    while block_rows > 1024 and block_rows % 2 == 0:
        block_rows = block_rows // 2
    return block_rows


def adam_update(item_grad, moment, second, table):
    new_moment = first_decay * moment + (1.0 - first_decay) * item_grad
    new_second = second_decay * second + (1.0 - second_decay) * jnp.mean(
        item_grad * item_grad, axis=1
    )
    new_table = (
        table.astype(jnp.float32)
        - step_rate * new_moment / (jnp.sqrt(new_second) + epsilon)[:, None]
    ).astype(jnp.bfloat16)
    return (new_table, new_moment, new_second)


def body(events_x, proj, out_grad, block_mask, item_ids, owner_of, local_of, table, moment, second):
    tokens = events_x.shape[1]
    features = events_x.shape[2]
    head_size = features // HEADS
    seq_count = lax.axis_size("seq")
    owner_count = lax.axis_size("table")
    position = lax.axis_index("seq")
    history_scale = 1.0 / math.sqrt(tokens * seq_count)
    temper = 1.0 / math.sqrt(head_size)
    block_ids = jnp.arange(seq_count)
    inputs = events_x[0]
    cotangent = out_grad[0]
    projected = jnp.dot(inputs, proj, preferred_element_type=jnp.float32).astype(jnp.bfloat16)
    queries = projected[:, :features]
    key_mat = projected[:, features : 2 * features]
    value_mat = projected[:, 2 * features :]
    own_pos = position * tokens + jnp.arange(tokens)
    visible_col = lax.dynamic_slice_in_dim(block_mask, position, 1, 1)[:, 0]

    def split_heads(matrix):
        return matrix.reshape(matrix.shape[0], HEADS, head_size)

    def pair_terms(query_block, grad_block, key_block, value_block, allowed):
        scores = (
            jnp.einsum(
                "qhe,khe->hqk",
                split_heads(query_block),
                split_heads(key_block),
                preferred_element_type=jnp.float32,
            )
            * temper
        )
        gates = jax.nn.sigmoid(scores)
        weights = (scores * gates * history_scale * allowed).astype(jnp.bfloat16)
        slopes = gates * (1.0 + scores * (1.0 - gates))
        attn_grad = jnp.einsum(
            "qhe,khe->hqk",
            split_heads(grad_block),
            split_heads(value_block),
            preferred_element_type=jnp.float32,
        )
        score_grad = (attn_grad * slopes * (history_scale * temper) * allowed).astype(jnp.bfloat16)
        return (weights, score_grad)

    zero_rows = jnp.zeros((tokens, features), jnp.float32)
    zero_terms = jnp.zeros((tokens * seq_count, features), jnp.float32)
    query_piece = lax.all_gather(queries, "seq", axis=0, tiled=True)
    grad_piece = lax.all_gather(cotangent, "seq", axis=0, tiled=True)
    block_rows = block_length(query_piece.shape[0])

    def advance(block_index, running):
        first_row = block_index * block_rows
        query_block = lax.dynamic_slice_in_dim(query_piece, first_row, block_rows, 0)
        grad_block = lax.dynamic_slice_in_dim(grad_piece, first_row, block_rows, 0)
        query_pos = first_row + jnp.arange(block_rows)
        query_blk = query_pos // tokens
        visible = jnp.any(
            (query_blk[:, None] == block_ids[None, :]) & (visible_col[None, :] == 1), axis=1
        ) | (query_blk == position)
        allowed = (visible[:, None] & (own_pos[None, :] <= query_pos[:, None])).astype(jnp.float32)

        def accumulate(current):
            weights, score_grad = pair_terms(query_block, grad_block, key_mat, value_mat, allowed)
            value_total = current[1] + jnp.einsum(
                "hqk,qhe->khe", weights, split_heads(grad_block), preferred_element_type=jnp.float32
            ).reshape(tokens, features)
            key_total = current[0] + jnp.einsum(
                "hqk,qhe->khe",
                score_grad,
                split_heads(query_block),
                preferred_element_type=jnp.float32,
            ).reshape(tokens, features)
            query_part = jnp.einsum(
                "hqk,khe->qhe", score_grad, split_heads(key_mat), preferred_element_type=jnp.float32
            ).reshape(block_rows, features)
            query_terms = lax.dynamic_update_slice(
                current[2], query_part, (first_row, jnp.int32(0))
            )
            return (key_total, value_total, query_terms)

        return lax.cond(jnp.any(allowed > 0), accumulate, lambda current: current, running)

    key_grad, value_grad, query_terms = lax.fori_loop(
        0, query_piece.shape[0] // block_rows, advance, (zero_rows, zero_rows, zero_terms)
    )
    query_grad = lax.psum_scatter(query_terms, "seq", scatter_dimension=0, tiled=True)
    stacked = jnp.concatenate([query_grad, key_grad, value_grad], axis=1).astype(jnp.bfloat16)
    input_grad = lax.dot_general(
        stacked, proj, (((1,), (1,)), ((), ())), preferred_element_type=jnp.float32
    ).astype(jnp.bfloat16)
    event_items = item_ids[0]
    owners = owner_of[event_items]
    slab_index = local_of[event_items]
    capacity = 2 * tokens // owner_count
    owner_hits = (owners[:, None] == jnp.arange(owner_count)[None, :]).astype(jnp.int32)
    slots = jnp.sum(jnp.cumsum(owner_hits, axis=0) * owner_hits, axis=1) - 1
    target = owners * capacity + slots
    send_rows = (
        jnp.zeros((owner_count * capacity, features), jnp.bfloat16)
        .at[target]
        .set(input_grad)
        .reshape(owner_count, capacity, features)
    )
    send_index = (
        jnp.full((owner_count * capacity,), -1, jnp.int32)
        .at[target]
        .set(slab_index)
        .reshape(owner_count, capacity)
    )
    got_rows, got_index = (
        lax.all_to_all(send_rows, "table", split_axis=0, concat_axis=0, tiled=True),
        lax.all_to_all(send_index, "table", split_axis=0, concat_axis=0, tiled=True),
    )
    slab_rows = table.shape[0]
    select = (got_index.reshape(-1)[None, :] == jnp.arange(slab_rows)[:, None]).astype(jnp.bfloat16)
    slab_grad = jnp.dot(select, got_rows.reshape(-1, features), preferred_element_type=jnp.float32)
    item_grad = lax.psum(slab_grad.astype(jnp.bfloat16), "seq").astype(jnp.float32)
    new_table, new_moment, new_second = adam_update(item_grad, moment, second, table)
    clamped = jnp.clip(got_index, 0, slab_rows - 1)
    replies = jnp.where(
        (got_index >= 0)[:, :, None], new_table[clamped], jnp.zeros((), jnp.bfloat16)
    )
    returned_rows = lax.all_to_all(replies, "table", split_axis=0, concat_axis=0, tiled=True)
    event_rows = returned_rows.reshape(owner_count * capacity, features)[target]
    return (new_table, new_moment, new_second, event_rows[None])


def solution(mesh):
    return jax.shard_map(
        body,
        mesh=mesh,
        in_specs=(
            P("table", "seq", None),
            P(),
            P("table", "seq", None),
            P(),
            P("table", "seq"),
            P(),
            P(),
            P("table", None),
            P("table", None),
            P("table"),
        ),
        out_specs=(P("table", None), P("table", None), P("table"), P("table", "seq", None)),
        check_vma=False,
    )
```

profile of v0, /device:TPU:1, one launch (start us, length us, event | category | flops | bytes accessed | tf_op | source)
XLA Modules:
  0.0 459.3 jit_solution(3907325187602014289)
XLA Ops:
  10.6 1.7 copy.42
  13.5 62.1 %all-gather.4.cloned.1.call-done = bf16[2048,512]{1,0:T(8,128)(2,1)} async-done(((bf16[128,512]{1,0:T(8,128)(2,1)}), bf16[2048,512]{1,0:T(8,128)(2,1)}) %all-gather.4.cloned.1.call-update) | async-done | bytes 2097168 | tf_op jit(solution)/shard_map/all_gather | solution.py:79
  75.5 4.0 copy.44
  79.5 61.6 %all-gather.6.cloned.1.call-done = bf16[1,2048,512]{1,2,0:T(8,128)(2,1)} async-done(((bf16[1,128,512]{1,2,0:T(8,128)(2,1)}), bf16[1,2048,512]{1,2,0:T(8,128)(2,1)}) %all-gather.6.cloned.1.call-update) | async-done | bytes 2097168 | tf_op jit(solution)/shard_map/all_gather | solution.py:80
  141.1 2.5 broadcast_in_dim.58
  143.6 27.1 %while.20 = (s32[]{:T(128)}, f32[128,512]{0,1:T(8,128)S(1)}, f32[128,512]{0,1:T(8,128)S(1)}, f32[2048,512]{0,1:T(8,128)}, s32[16,1]{0,1:T(1,128)S(1)}, /*index=5...) while((s32[]{:T(128)}, f32[128,512]{0,1:T(8,128)S(1)}, ...), condition=%wide.region_8.9_spmd.clone, body=%wide.region_3.8_spmd.clone.sunk | while | flops 691094656 | bytes 72766960 | solution.py:115
  145.4 11.8 %conditional.3 = ((f32[128,512]{0,1:T(8,128)S(1)}, f32[128,512]{0,1:T(8,128)S(1)}, f32[2048,512]{0,1:T(8,128)})) conditional(s32[]{:T(128)} %convert_element_type.86, (f32[128,512]{0,1:T(8,128)S(1)}, f32[128,512]{0,1:T(8,128)S(1)}, f32[2048,512]{0,1:T(8,128)}) %tuple.80, (s32[]{:T(128)}, bf16[2048,512]{0,1:T(8,128)(2,1)}, ...), branch_computations={%region_6.6_spmd, %region_7.7_spmd} | conditional | flops 690356224 | bytes 72220808 | solution.py:113
  148.9 1.4 fusion.4
  150.3 2.4 multiply_convert_fusion.1
  155.2 1.9 copy-done.2
  158.9 11.8 %conditional.3 = ((f32[128,512]{0,1:T(8,128)S(1)}, f32[128,512]{0,1:T(8,128)S(1)}, f32[2048,512]{0,1:T(8,128)})) conditional(s32[]{:T(128)} %convert_element_type.86, (f32[128,512]{0,1:T(8,128)S(1)}, f32[128,512]{0,1:T(8,128)S(1)}, f32[2048,512]{0,1:T(8,128)}) %tuple.80, (s32[]{:T(128)}, bf16[2048,512]{0,1:T(8,128)(2,1)}, ...), branch_computations={%region_6.6_spmd, %region_7.7_spmd} | conditional | flops 690356224 | bytes 72220808 | solution.py:113
  162.4 1.4 fusion.4
  163.9 2.4 multiply_convert_fusion.1
  168.7 1.9 copy-done.2
  176.0 14.4 %all-to-all-start = ((s32[32,1,8]{2,1,0:T(1,128)}), s32[32,1,8]{2,1,0:T(1,128)S(1)}, u32[]{:S(2)}, u32[]{:S(2)}) async-start(s32[32,1,8]{2,1,0:T(1,128)} %bitcast.14), calls=%async_computation | async-start | bytes 32768 | tf_op jit(solution)/shard_map/all_to_all | solution.py:144
  190.4 72.2 %reduce-scatter.2.cloned.1.call-done = f32[128,512]{0,1:T(8,128)} async-done(((f32[2048,512]{0,1:T(8,128)}), f32[128,512]{0,1:T(8,128)}) %reduce-scatter.2.cloned.1.call-update) | async-done | bytes 262160 | tf_op jit(solution)/shard_map/reduce_scatter | solution.py:118
  264.2 1.7 scatter_custom_fusion.1
  265.9 14.8 %all-to-all-start.1 = ((bf16[32,8,512]{2,1,0:T(8,128)(2,1)}), bf16[32,8,512]{2,1,0:T(8,128)(2,1)S(1)}, u32[]{:S(2)}, u32[]{:S(2)}) async-start(bf16[32,8,512]{2,1,0:T(8,128)(2,1)} %bitcast.17), calls=%async_computation.2 | async-start | bytes 524288 | tf_op jit(solution)/shard_map/all_to_all | solution.py:143
  282.2 20.8 %all-to-all-done.1 = bf16[32,8,512]{2,1,0:T(8,128)(2,1)S(1)} async-done(((bf16[32,8,512]{2,1,0:T(8,128)(2,1)}), bf16[32,8,512]{2,1,0:T(8,128)(2,1)S(1)}, u32[]{:S(2)}, u32[]{:S(2)}) %all-to-all-start.1) | async-done | bytes 262176 | tf_op jit(solution)/shard_map/all_to_all | solution.py:143
  304.4 103.3 %all-reduce.2.cloned.1.call-done = bf16[512,512]{1,0:T(8,128)(2,1)} async-done(((bf16[512,512]{1,0:T(8,128)(2,1)}), bf16[512,512]{1,0:T(8,128)(2,1)}) %all-reduce.2.cloned.1.call-update) | async-done | bytes 524304 | tf_op jit(solution)/shard_map/psum | solution.py:149
  409.6 2.5 subtract_convert_fusion
  414.0 15.0 %all-to-all-start.2 = ((bf16[32,8,512]{2,1,0:T(8,128)(2,1)}), bf16[32,8,512]{2,1,0:T(8,128)(2,1)S(1)}, u32[]{:S(2)}, u32[]{:S(2)}) async-start(bf16[32,8,512]{2,1,0:T(8,128)(2,1)} %bitcast_select_fusion), calls=%async_computation.3 | async-start | bytes 524288 | tf_op jit(solution)/shard_map/all_to_all | solution.py:155
  429.0 22.2 %all-to-all-done.2 = bf16[32,8,512]{2,1,0:T(8,128)(2,1)S(1)} async-done(((bf16[32,8,512]{2,1,0:T(8,128)(2,1)}), bf16[32,8,512]{2,1,0:T(8,128)(2,1)S(1)}, u32[]{:S(2)}, u32[]{:S(2)}) %all-to-all-start.2) | async-done | bytes 262176 | tf_op jit(solution)/shard_map/all_to_all | solution.py:155
  451.3 1.5 gather_fusion.3
  (95 shorter events, 32.2 us)
Async XLA Ops:
  7.2 1.4 copy-start
  7.2 68.4 %all-gather.4.cloned.1.call-start = ((), (), s32[]{:S(2)}) async-start(), calls=%async_computation.4 | async-start | bytes 2228224 | tf_op jit(solution)/shard_map/all_gather | solution.py:79
  10.6 130.5 %all-gather.6.cloned.1.call-start = ((), (), s32[]{:S(2)}) async-start(), calls=%async_computation.7 | async-start | bytes 2228224 | tf_op jit(solution)/shard_map/all_gather | solution.py:80
  12.3 250.2 %reduce-scatter.2.cloned.1.call-start = ((), (), s32[]{:S(2)}) async-start(), calls=%async_computation.5 | async-start | bytes 4456448 | tf_op jit(solution)/shard_map/reduce_scatter | solution.py:118
  152.7 2.2 copy-start.1
  155.2 2.0 copy-start.2
  166.2 2.2 copy-start.1
  168.7 2.0 copy-start.2
  170.7 0.7 copy-start.8
  170.7 0.9 copy-start.4
  170.7 2.3 copy-start.5
  171.3 237.6 %copy-start.7 = (f32[512]{0:T(512)S(1)}, f32[512]{0:T(512)}, u32[]{:S(2)}) copy-start(f32[512]{0:T(512)} %param.23) | copy-start | bytes 6148
  171.3 238.2 %copy-start.6 = (f32[512,512]{1,0:T(8,128)S(1)}, f32[512,512]{1,0:T(8,128)}, u32[]{:S(2)}) copy-start(f32[512,512]{1,0:T(8,128)} %param.22) | copy-start | bytes 3145732
  176.0 89.9 %all-to-all-start = ((s32[32,1,8]{2,1,0:T(1,128)}), s32[32,1,8]{2,1,0:T(1,128)S(1)}, u32[]{:S(2)}, u32[]{:S(2)}) async-start(s32[32,1,8]{2,1,0:T(1,128)} %bitcast.14), calls=%async_computation | async-start | bytes 32768 | tf_op jit(solution)/shard_map/all_to_all | solution.py:144
  265.9 37.1 %all-to-all-start.1 = ((bf16[32,8,512]{2,1,0:T(8,128)(2,1)}), bf16[32,8,512]{2,1,0:T(8,128)(2,1)S(1)}, u32[]{:S(2)}, u32[]{:S(2)}) async-start(bf16[32,8,512]{2,1,0:T(8,128)(2,1)} %bitcast.17), calls=%async_computation.2 | async-start | bytes 524288 | tf_op jit(solution)/shard_map/all_to_all | solution.py:143
  280.7 127.0 %all-reduce.2.cloned.1.call-start = ((), (), s32[]{:S(2)}) async-start(), calls=%async_computation.6 | async-start | bytes 1048576 | tf_op jit(solution)/shard_map/psum | solution.py:149
  412.1 40.7 %copy-start.3 = (bf16[512,512]{1,0:T(8,128)(2,1)}, bf16[512,512]{1,0:T(8,128)(2,1)S(1)}, u32[]{:S(2)}) copy-start(bf16[512,512]{1,0:T(8,128)(2,1)S(1)} %get-tuple-element.535) | copy-start | bytes 1572868
  414.0 37.2 %all-to-all-start.2 = ((bf16[32,8,512]{2,1,0:T(8,128)(2,1)}), bf16[32,8,512]{2,1,0:T(8,128)(2,1)S(1)}, u32[]{:S(2)}, u32[]{:S(2)}) async-start(bf16[32,8,512]{2,1,0:T(8,128)(2,1)} %bitcast_select_fusion), calls=%async_computation.3 | async-start | bytes 524288 | tf_op jit(solution)/shard_map/all_to_all | solution.py:155
Sparse Core Ops, SparseCore 0:
  11.6 63.9 all-gather.3
  79.1 61.9 all-gather.5
  170.8 91.6 reduce-scatter.1
  304.3 103.4 all-reduce.1
where the time goes:
time: 460 us; the launch traced here: 459 us
  waiting for transfers between devices  342 us (74%)
  starting transfers between devices  44.3 us (10%)
  local copies, waits for them, and re-layouts  32.5 us (7%)
  matrix products  14.9 us (3%)
  between operations  14 us (3%)
  other arithmetic  9.82 us (2%)
    psum x1, waiting for transfers between devices, body(): lax.psum(slab_grad.astype(jnp.bfloat16), 'seq').astype(jnp.float32)  103 us
    reduce_scatter x1, waiting for transfers between devices, body(): lax.psum_scatter(query_terms, 'seq', scatter_dimension=0, tiled=True)  72.2 us
    all_gather x1, waiting for transfers between devices, body(): query_piece = lax.all_gather(queries, 'seq', axis=0, tiled=True)  62.1 us
    all_gather x1, waiting for transfers between devices, body(): grad_piece = lax.all_gather(cotangent, 'seq', axis=0, tiled=True)  61.6 us
    all_to_all x1, waiting for transfers between devices, body(): lax.all_to_all(replies, 'table', split_axis=0, concat_axis=0, tiled=True)  22.2 us
    all_to_all x1, waiting for transfers between devices, body(): lax.all_to_all(send_rows, 'table', split_axis=0, concat_axis=0, tiled=True)  20.8 us
    all_to_all x1, starting transfers between devices, body(): lax.all_to_all(replies, 'table', split_axis=0, concat_axis=0, tiled=True)  15 us
    all_to_all x1, starting transfers between devices, body(): lax.all_to_all(send_rows, 'table', split_axis=0, concat_axis=0, tiled=True)  14.8 us
  transfers between devices with their start and end apart: 7, of which 6 were waited for; matrix products, arithmetic and copies ran while one was open for 3% of the time, Pallas kernels for 0%

commit v1 on v0

--- a/solution.py
+++ b/solution.py
@@ -9,6 +9,11 @@
 second_decay = 0.99
 step_rate = 0.05
 epsilon = 1e-08
+
+
+def add_all(x, axis):
+    shards = lax.all_gather(x, axis)
+    return jnp.sum(shards, axis=0)
 
 
 def block_length(piece_rows):
@@ -146,7 +151,7 @@
     slab_rows = table.shape[0]
     select = (got_index.reshape(-1)[None, :] == jnp.arange(slab_rows)[:, None]).astype(jnp.bfloat16)
     slab_grad = jnp.dot(select, got_rows.reshape(-1, features), preferred_element_type=jnp.float32)
-    item_grad = lax.psum(slab_grad.astype(jnp.bfloat16), "seq").astype(jnp.float32)
+    item_grad = add_all(slab_grad.astype(jnp.bfloat16), "seq").astype(jnp.float32)
     new_table, new_moment, new_second = adam_update(item_grad, moment, second, table)
     clamped = jnp.clip(got_index, 0, slab_rows - 1)
     replies = jnp.where(

time: 460 us -> 434 us (0.943)
  waiting for transfers between devices: 342 us -> 314 us
    psum x1 -> x0, waiting for transfers between devices: 103 us -> none  [body(): lax.psum(slab_grad.astype(jnp.bfloat16), 'seq').astype(jnp.float32)]
    all_gather x0 -> x1, waiting for transfers between devices: none -> 74.8 us  [add_all(): shards = lax.all_gather(x, axis)]
    reduce_sum x0 -> x1, other arithmetic: none -> 4.88 us  [add_all(): return jnp.sum(shards, axis=0)]
  transfers between devices with their start and end apart: 7 -> 7, of which waited for: 6 -> 6; matrix products, arithmetic and copies ran while one was open for 3% -> 4% of each run, Pallas kernels for 0% -> 0%
where the time goes in v1:
time: 434 us; the launch traced here: 433 us
  waiting for transfers between devices  314 us (72%)
  starting transfers between devices  42.7 us (10%)
  local copies, waits for them, and re-layouts  32.5 us (7%)
  matrix products  14.9 us (3%)
  between operations  14 us (3%)
  other arithmetic  13.7 us (3%)
    all_gather x1, waiting for transfers between devices, add_all(): shards = lax.all_gather(x, axis)  74.8 us
    reduce_scatter x1, waiting for transfers between devices, body(): lax.psum_scatter(query_terms, 'seq', scatter_dimension=0, tiled=True)  72.2 us
    all_gather x1, waiting for transfers between devices, body(): query_piece = lax.all_gather(queries, 'seq', axis=0, tiled=True)  62.1 us
    all_gather x1, waiting for transfers between devices, body(): grad_piece = lax.all_gather(cotangent, 'seq', axis=0, tiled=True)  61.6 us
    all_to_all x1, waiting for transfers between devices, body(): lax.all_to_all(replies, 'table', split_axis=0, concat_axis=0, tiled=True)  22.2 us
    all_to_all x1, waiting for transfers between devices, body(): lax.all_to_all(send_rows, 'table', split_axis=0, concat_axis=0, tiled=True)  20.7 us
    all_to_all x1, starting transfers between devices, body(): lax.all_to_all(send_rows, 'table', split_axis=0, concat_axis=0, tiled=True)  14.8 us
    all_to_all x1, starting transfers between devices, body(): lax.all_to_all(send_index, 'table', split_axis=0, concat_axis=0, tiled=True)  14.4 us
  transfers between devices with their start and end apart: 7, of which 6 were waited for; matrix products, arithmetic and copies ran while one was open for 4% of the time, Pallas kernels for 0%

profile of v1, /device:TPU:1, one launch (start us, length us, event | category | flops | bytes accessed | tf_op | source)
XLA Modules:
  0.0 433.0 jit_solution(12166473410530913612)
XLA Ops:
  10.6 1.7 copy.42
  13.5 62.1 %all-gather.6.cloned.1.call-done = bf16[2048,512]{1,0:T(8,128)(2,1)} async-done(((bf16[128,512]{1,0:T(8,128)(2,1)}), bf16[2048,512]{1,0:T(8,128)(2,1)}) %all-gather.6.cloned.1.call-update) | async-done | bytes 2097168 | tf_op jit(solution)/shard_map/all_gather | solution.py:84
  75.5 4.0 copy.44
  79.5 61.6 %all-gather.8.cloned.1.call-done = bf16[1,2048,512]{1,2,0:T(8,128)(2,1)} async-done(((bf16[1,128,512]{1,2,0:T(8,128)(2,1)}), bf16[1,2048,512]{1,2,0:T(8,128)(2,1)}) %all-gather.8.cloned.1.call-update) | async-done | bytes 2097168 | tf_op jit(solution)/shard_map/all_gather | solution.py:85
  141.1 2.5 broadcast_in_dim.58
  143.6 27.1 %while.20 = (s32[]{:T(128)}, f32[128,512]{0,1:T(8,128)S(1)}, f32[128,512]{0,1:T(8,128)S(1)}, f32[2048,512]{0,1:T(8,128)}, s32[16,1]{0,1:T(1,128)S(1)}, /*index=5...) while((s32[]{:T(128)}, f32[128,512]{0,1:T(8,128)S(1)}, ...), condition=%wide.region_8.9_spmd.clone, body=%wide.region_3.8_spmd.clone.sunk | while | flops 691094656 | bytes 72766960 | solution.py:120
  145.4 11.8 %conditional.3 = ((f32[128,512]{0,1:T(8,128)S(1)}, f32[128,512]{0,1:T(8,128)S(1)}, f32[2048,512]{0,1:T(8,128)})) conditional(s32[]{:T(128)} %convert_element_type.88, (f32[128,512]{0,1:T(8,128)S(1)}, f32[128,512]{0,1:T(8,128)S(1)}, f32[2048,512]{0,1:T(8,128)}) %tuple.80, (s32[]{:T(128)}, bf16[2048,512]{0,1:T(8,128)(2,1)}, ...), branch_computations={%region_6.6_spmd, %region_7.7_spmd} | conditional | flops 690356224 | bytes 72220808 | solution.py:118
  150.3 2.4 multiply_convert_fusion.1
  155.2 1.9 copy-done.2
  158.9 11.8 %conditional.3 = ((f32[128,512]{0,1:T(8,128)S(1)}, f32[128,512]{0,1:T(8,128)S(1)}, f32[2048,512]{0,1:T(8,128)})) conditional(s32[]{:T(128)} %convert_element_type.88, (f32[128,512]{0,1:T(8,128)S(1)}, f32[128,512]{0,1:T(8,128)S(1)}, f32[2048,512]{0,1:T(8,128)}) %tuple.80, (s32[]{:T(128)}, bf16[2048,512]{0,1:T(8,128)(2,1)}, ...), branch_computations={%region_6.6_spmd, %region_7.7_spmd} | conditional | flops 690356224 | bytes 72220808 | solution.py:118
  162.5 1.4 fusion.4
  163.9 2.4 multiply_convert_fusion.1
  168.7 1.9 copy-done.2
  176.0 14.4 %all-to-all-start = ((s32[32,1,8]{2,1,0:T(1,128)}), s32[32,1,8]{2,1,0:T(1,128)S(1)}, u32[]{:S(2)}, u32[]{:S(2)}) async-start(s32[32,1,8]{2,1,0:T(1,128)} %bitcast.14), calls=%async_computation | async-start | bytes 32768 | tf_op jit(solution)/shard_map/all_to_all | solution.py:149
  190.4 72.2 %reduce-scatter.2.cloned.1.call-done = f32[128,512]{0,1:T(8,128)} async-done(((f32[2048,512]{0,1:T(8,128)}), f32[128,512]{0,1:T(8,128)}) %reduce-scatter.2.cloned.1.call-update) | async-done | bytes 262160 | tf_op jit(solution)/shard_map/reduce_scatter | solution.py:123
  264.2 1.7 scatter_custom_fusion.1
  266.0 14.8 %all-to-all-start.1 = ((bf16[32,8,512]{2,1,0:T(8,128)(2,1)}), bf16[32,8,512]{2,1,0:T(8,128)(2,1)S(1)}, u32[]{:S(2)}, u32[]{:S(2)}) async-start(bf16[32,8,512]{2,1,0:T(8,128)(2,1)} %bitcast.17), calls=%async_computation.2 | async-start | bytes 524288 | tf_op jit(solution)/shard_map/all_to_all | solution.py:148
  282.3 20.7 %all-to-all-done.1 = bf16[32,8,512]{2,1,0:T(8,128)(2,1)S(1)} async-done(((bf16[32,8,512]{2,1,0:T(8,128)(2,1)}), bf16[32,8,512]{2,1,0:T(8,128)(2,1)S(1)}, u32[]{:S(2)}, u32[]{:S(2)}) %all-to-all-start.1) | async-done | bytes 262176 | tf_op jit(solution)/shard_map/all_to_all | solution.py:148
  304.6 74.8 %all-gather.10.cloned.1.call-done = bf16[8192,512]{1,0:T(8,128)(2,1)} async-done(((bf16[512,512]{1,0:T(8,128)(2,1)}), bf16[8192,512]{1,0:T(8,128)(2,1)}) %all-gather.10.cloned.1.call-update) | async-done | bytes 8388624 | tf_op jit(solution)/shard_map/all_gather | solution.py:15
  379.4 4.9 %reduce_sum.31 = bf16[512,512]{1,0:T(8,128)(2,1)S(1)} reduce(bf16[16,512,512]{2,1,0:T(8,128)(2,1)} %bitcast.66, bf16[]{:T(256)} %constant.177.clone.1), dimensions={0}, to_apply=%region_11.12 | reduce | flops 3932160 | bytes 8912898 | tf_op jit(solution)/shard_map/reduce_sum | solution.py:16
  385.0 2.5 subtract_convert_fusion
  389.5 13.2 %all-to-all-start.2 = ((bf16[32,8,512]{2,1,0:T(8,128)(2,1)}), bf16[32,8,512]{2,1,0:T(8,128)(2,1)S(1)}, u32[]{:S(2)}, u32[]{:S(2)}) async-start(bf16[32,8,512]{2,1,0:T(8,128)(2,1)} %bitcast_select_fusion), calls=%async_computation.3 | async-start | bytes 524288 | tf_op jit(solution)/shard_map/all_to_all | solution.py:160
  402.7 22.2 %all-to-all-done.2 = bf16[32,8,512]{2,1,0:T(8,128)(2,1)S(1)} async-done(((bf16[32,8,512]{2,1,0:T(8,128)(2,1)}), bf16[32,8,512]{2,1,0:T(8,128)(2,1)S(1)}, u32[]{:S(2)}, u32[]{:S(2)}) %all-to-all-start.2) | async-done | bytes 262176 | tf_op jit(solution)/shard_map/all_to_all | solution.py:160
  425.0 1.5 gather_fusion.3
  (96 shorter events, 32.8 us)
Async XLA Ops:
  7.2 1.4 copy-start
  7.2 68.4 %all-gather.6.cloned.1.call-start = ((), (), s32[]{:S(2)}) async-start(), calls=%async_computation.4 | async-start | bytes 2228224 | tf_op jit(solution)/shard_map/all_gather | solution.py:84
  10.6 130.5 %all-gather.8.cloned.1.call-start = ((), (), s32[]{:S(2)}) async-start(), calls=%async_computation.6 | async-start | bytes 2228224 | tf_op jit(solution)/shard_map/all_gather | solution.py:85
  12.3 250.3 %reduce-scatter.2.cloned.1.call-start = ((), (), s32[]{:S(2)}) async-start(), calls=%async_computation.5 | async-start | bytes 4456448 | tf_op jit(solution)/shard_map/reduce_scatter | solution.py:123
  152.7 2.2 copy-start.1
  155.2 2.0 copy-start.2
  166.2 2.2 copy-start.1
  168.7 2.0 copy-start.2
  170.7 0.7 copy-start.8
  170.7 0.9 copy-start.4
  170.7 2.3 copy-start.5
  176.0 90.0 %all-to-all-start = ((s32[32,1,8]{2,1,0:T(1,128)}), s32[32,1,8]{2,1,0:T(1,128)S(1)}, u32[]{:S(2)}, u32[]{:S(2)}) async-start(s32[32,1,8]{2,1,0:T(1,128)} %bitcast.14), calls=%async_computation | async-start | bytes 32768 | tf_op jit(solution)/shard_map/all_to_all | solution.py:149
  266.0 37.1 %all-to-all-start.1 = ((bf16[32,8,512]{2,1,0:T(8,128)(2,1)}), bf16[32,8,512]{2,1,0:T(8,128)(2,1)S(1)}, u32[]{:S(2)}, u32[]{:S(2)}) async-start(bf16[32,8,512]{2,1,0:T(8,128)(2,1)} %bitcast.17), calls=%async_computation.2 | async-start | bytes 524288 | tf_op jit(solution)/shard_map/all_to_all | solution.py:148
  280.8 98.6 %all-gather.10.cloned.1.call-start = ((), (), s32[]{:S(2)}) async-start(), calls=%async_computation.7 | async-start | bytes 8912896 | tf_op jit(solution)/shard_map/all_gather | solution.py:15
  379.4 5.1 %copy-start.7 = (f32[512]{0:T(512)S(1)}, f32[512]{0:T(512)}, u32[]{:S(2)}) copy-start(f32[512]{0:T(512)} %param.23) | copy-start | bytes 6148
  379.4 5.7 %copy-start.6 = (bf16[512,512]{1,0:T(8,128)(2,1)S(1)}, bf16[512,512]{1,0:T(8,128)(2,1)}, u32[]{:S(2)}) copy-start(bf16[512,512]{1,0:T(8,128)(2,1)} %param.21) | copy-start | bytes 1572868
  387.6 38.9 %copy-start.3 = (bf16[512,512]{1,0:T(8,128)(2,1)}, bf16[512,512]{1,0:T(8,128)(2,1)S(1)}, u32[]{:S(2)}) copy-start(bf16[512,512]{1,0:T(8,128)(2,1)S(1)} %get-tuple-element.535) | copy-start | bytes 1572868
  389.5 35.4 %all-to-all-start.2 = ((bf16[32,8,512]{2,1,0:T(8,128)(2,1)}), bf16[32,8,512]{2,1,0:T(8,128)(2,1)S(1)}, u32[]{:S(2)}, u32[]{:S(2)}) async-start(bf16[32,8,512]{2,1,0:T(8,128)(2,1)} %bitcast_select_fusion), calls=%async_computation.3 | async-start | bytes 524288 | tf_op jit(solution)/shard_map/all_to_all | solution.py:160
Sparse Core Ops, SparseCore 0:
  11.6 63.9 all-gather.5
  79.1 61.9 all-gather.7
  170.8 91.7 reduce-scatter.1
  304.3 75.0 all-gather.9
